TPU v7x, 32 devices: a whole 2x2x4 slice. The times are simulated.
32 devices in a mesh: groups: 2 (over x), ctx: 8 (over z, y), tp: 2 (over core).
Axes of the slice: x: 2, y: 2, z: 4, core: 2. Of those that a mesh axis runs over, the one named last changes fastest.
Arguments:
- enc_input: bfloat16 [2048, 4096], P(('groups', 'ctx')), parts along dimension 0, may hold values from -6 to 6
- enc_query: bfloat16 [2048, 1024], P(('groups', 'ctx'), 'tp'), parts along dimension 0
- enc_key: bfloat16 [2048, 1024], P(('groups', 'ctx'), 'tp'), parts along dimension 0
- enc_value: bfloat16 [2048, 1024], P(('groups', 'ctx'), 'tp'), parts along dimension 0, may hold values from -6 to 6
- seq_length: int32 [2], P('groups'), parts along dimension 0, may hold values from 256 to 1024
- attn_out_weight: bfloat16 [1024, 4096], P('tp'), may hold values from -0.1875 to 0.1875
- enc_gain: bfloat16 [4096], replicated, may hold values from 0.25 to 1.75
- cross_key_weight: bfloat16 [4096, 1024], P('ctx', 'tp'), may hold values from -0.09375 to 0.09375
- cross_value_weight: bfloat16 [4096, 1024], P('ctx', 'tp'), may hold values from -0.09375 to 0.09375
- embed_table: bfloat16 [32128, 4096], P('tp', 'ctx')
- dec_ids: int32 [32, 2], P('groups'), parts along dimension 0, may hold values from 0 to 32127
- dec_gain: bfloat16 [4096], P('ctx'), may hold values from 0.25 to 1.75
- cross_query_weight: bfloat16 [4096, 1024], P('ctx', 'tp')
- cross_out_weight: bfloat16 [1024, 4096], P('tp', 'ctx'), may hold values from -0.1875 to 0.1875
Outputs:
- cross_keys: bfloat16 [16, 128, 1024], P(('groups', 'ctx'), None, 'tp'), parts along dimension 0
- cross_values: bfloat16 [16, 128, 1024], P(('groups', 'ctx'), None, 'tp'), parts along dimension 0
- decoded: bfloat16 [32, 2, 4096], P('groups', None, 'ctx'), parts along dimension 0
There are 2 independent parts, one for each index of `groups`. A program takes and returns all parts, laid end to end along the dimension named above; an argument that names none is the same for every part. Nothing has to cross between parts.
Inputs may be any that keep to these rules, and one draw needn't show every extreme that they name: `seq_length`: the input's real length.
All inputs are finite; a program needn't handle non-finite values.
Results may differ from a plain program's by a relative error of at most 0.04.
Values may be sent and summed in bfloat16 or wider, within the bound.
A program may use at most 128 MiB of HBM per device.

v0:
```python
import math

import jax
import jax.numpy as jnp
from jax import lax
from jax.sharding import PartitionSpec as P

D = 4096
HD = 128


EPSILON = 1e-06
FLOOR = -1e30


def joined(value, axis, join):
    pieces = jax.tree.map(lambda part: lax.all_gather(part, axis), value)
    head = jax.tree.map(lambda part: part[0], pieces)
    tail = jax.tree.map(lambda part: part[1:], pieces)
    total, _ = lax.scan(lambda total, piece: (join(total, piece), None), head, tail)
    return total


def softmax_merge(first, second):
    top_first, total_first, mixed_first = first
    top_second, total_second, mixed_second = second
    top = jnp.maximum(top_first, top_second)
    weight_first = jnp.exp(top_first - top)
    weight_second = jnp.exp(top_second - top)
    total = total_first * weight_first + total_second * weight_second
    mixed = mixed_first * weight_first[..., None] + mixed_second * weight_second[..., None]
    return (top, total, mixed)


def partial_softmax(queries, keys, values, valid, factor):
    scores = jnp.einsum("qhd,khd->hqk", queries, keys, preferred_element_type=jnp.float32) * factor
    scores = jnp.where(valid[None, None, :], scores, FLOOR)
    top = jnp.max(scores, axis=-1)
    probs = jnp.where(valid[None, None, :], jnp.exp(scores - top[..., None]), 0.0)
    total = jnp.sum(probs, axis=-1)
    mixed = jnp.einsum(
        "hqk,khd->hqd", probs.astype(jnp.bfloat16), values, preferred_element_type=jnp.float32
    )
    return (top, total, mixed)


def norm_rows(resid, gain):
    scale = lax.rsqrt(jnp.mean(resid * resid, axis=-1, keepdims=True) + EPSILON)
    return (resid * scale * gain.astype(jnp.float32)).astype(jnp.bfloat16)


def local(
    enc_input,
    enc_query,
    enc_key,
    enc_value,
    seq_length,
    attn_out_weight,
    enc_gain,
    cross_key_weight,
    cross_value_weight,
    embed_table,
    dec_ids,
    dec_gain,
    cross_query_weight,
    cross_out_weight,
):
    rows, inner_local = enc_query.shape
    heads_local = inner_local // HD
    limit = seq_length[0]
    queries = enc_query.reshape(rows, heads_local, HD)
    start_state = (
        jnp.full((heads_local, rows), FLOOR, jnp.float32),
        jnp.zeros((heads_local, rows), jnp.float32),
        jnp.zeros((heads_local, rows, HD), jnp.float32),
    )
    carry = start_state
    key_rows = lax.all_gather(enc_key, "ctx", axis=0, tiled=True)
    value_rows = lax.all_gather(enc_value, "ctx", axis=0, tiled=True)
    count = key_rows.shape[0]
    block = math.gcd(count, 2048)
    blocks = count // block
    key_blocks = key_rows.reshape(blocks, block, heads_local, HD)
    value_blocks = value_rows.reshape(blocks, block, heads_local, HD)
    offsets = jnp.arange(blocks, dtype=jnp.int32) * block

    def one_block(state, item):
        key_block, value_block, offset = item
        positions = offset + jnp.arange(block, dtype=jnp.int32)
        update = partial_softmax(queries, key_block, value_block, positions < limit, HD ** (-0.5))
        return (softmax_merge(state, update), None)

    carry, unused = lax.scan(one_block, carry, (key_blocks, value_blocks, offsets))
    top, total, mixed = carry
    context = (
        jnp.transpose(mixed / total[..., None], (1, 0, 2))
        .reshape(rows, inner_local)
        .astype(jnp.bfloat16)
    )
    summed = lax.psum(jnp.dot(context, attn_out_weight, preferred_element_type=jnp.float32), "tp")
    memory = norm_rows(enc_input.astype(jnp.float32) + summed, enc_gain)
    ctx_count = lax.axis_size("ctx")
    slots = rows // ctx_count
    key_sum = jnp.dot(
        memory,
        lax.all_gather(cross_key_weight, "ctx", axis=0, tiled=True),
        preferred_element_type=jnp.float32,
    )
    value_sum = jnp.dot(
        memory,
        lax.all_gather(cross_value_weight, "ctx", axis=0, tiled=True),
        preferred_element_type=jnp.float32,
    )
    key_rows = key_sum.astype(jnp.bfloat16)
    value_rows = value_sum.astype(jnp.bfloat16)
    keys_moved, values_moved = (
        lax.all_to_all(
            key_rows.reshape(slots, ctx_count, inner_local),
            "ctx",
            split_axis=1,
            concat_axis=0,
            tiled=True,
        ),
        lax.all_to_all(
            value_rows.reshape(slots, ctx_count, inner_local),
            "ctx",
            split_axis=1,
            concat_axis=0,
            tiled=True,
        ),
    )
    keys_cache = keys_moved.reshape(rows, inner_local)
    values_cache = values_moved.reshape(rows, inner_local)
    beams = dec_ids.shape[0]
    vocab_local = embed_table.shape[0]
    flat_ids = dec_ids.reshape(-1) - lax.axis_index("tp") * vocab_local
    inside = (flat_ids >= 0) & (flat_ids < vocab_local)
    looked = jnp.take(embed_table, jnp.clip(flat_ids, 0, vocab_local - 1), axis=0)
    own_rows = jnp.where(inside[:, None], looked.astype(jnp.float32), 0.0)
    hidden = lax.psum(own_rows.astype(jnp.bfloat16), "tp").astype(jnp.float32)
    scaled = (hidden * dec_gain.astype(jnp.float32)).astype(jnp.bfloat16)
    raw_part = jnp.dot(scaled, cross_query_weight, preferred_element_type=jnp.float32)
    square_part = jnp.sum(hidden * hidden, axis=-1)
    raw, squares = lax.psum((raw_part, square_part), "ctx")
    factor = lax.rsqrt(squares / D + EPSILON)
    query = (raw * factor[:, None] * HD ** (-0.5)).astype(jnp.bfloat16).reshape(-1, heads_local, HD)
    positions = jnp.arange(rows, dtype=jnp.int32) * ctx_count + lax.axis_index("ctx")
    local_part = partial_softmax(
        query,
        keys_cache.reshape(rows, heads_local, HD),
        values_cache.reshape(rows, heads_local, HD),
        positions < limit,
        1.0,
    )
    top_all, total_all, mixed_all = joined(local_part, "ctx", softmax_merge)
    attn = (
        jnp.transpose(mixed_all / total_all[..., None], (1, 0, 2))
        .reshape(-1, inner_local)
        .astype(jnp.bfloat16)
    )
    out_part = jnp.dot(attn, cross_out_weight, preferred_element_type=jnp.float32)
    out = lax.psum(out_part, "tp")
    decoded = (out + hidden).astype(jnp.bfloat16).reshape(beams, 2, -1)
    return (keys_cache[None], values_cache[None], decoded)


def solution(mesh):
    placed = (
        P(("groups", "ctx"), None),
        P(("groups", "ctx"), "tp"),
        P(("groups", "ctx"), "tp"),
        P(("groups", "ctx"), "tp"),
        P("groups"),
        P("tp", None),
        P(),
        P("ctx", "tp"),
        P("ctx", "tp"),
        P("tp", "ctx"),
        P("groups", None),
        P("ctx"),
        P("ctx", "tp"),
        P("tp", "ctx"),
    )
    return jax.shard_map(
        local,
        mesh=mesh,
        in_specs=placed,
        out_specs=(
            P(("groups", "ctx"), None, "tp"),
            P(("groups", "ctx"), None, "tp"),
            P("groups", None, "ctx"),
        ),
        check_vma=False,
    )
```

profile of v0, /device:TPU:0, one launch (start us, length us, event | category | flops | bytes accessed | tf_op | source)
XLA Modules:
  0.0 454.3 jit_solution(15801881285562292397)
XLA Ops:
  7.2 1.7 copy.38
  9.0 0.7 all-gather.12.cloned.1.call-update
  10.4 42.3 %all-gather.10.cloned.1.call-done = bf16[1024,512]{0,1:T(8,128)(2,1)} async-done(((bf16[128,512]{0,1:T(8,128)(2,1)}), bf16[1024,512]{0,1:T(8,128)(2,1)}) %all-gather.10.cloned.1.call-update) | async-done | bytes 1048592 | tf_op jit(solution)/shard_map/all_gather | solution.py:78
  52.8 1.9 fusion.3
  54.6 0.6 fusion.4
  55.2 39.0 %all-gather.12.cloned.1.call-done = bf16[1024,512]{1,0:T(8,128)(2,1)} async-done(((bf16[128,512]{1,0:T(8,128)(2,1)}), bf16[1024,512]{1,0:T(8,128)(2,1)}) %all-gather.12.cloned.1.call-update) | async-done | bytes 1048592 | tf_op jit(solution)/shard_map/all_gather | solution.py:79
  94.2 2.3 copy.41
  96.5 2.1 fusion.9
  98.6 0.4 copy-done.3
  99.0 2.1 fusion.54
  101.1 0.5 all-gather.14.cloned.1.call-update
  101.7 0.5 all-gather.16.cloned.1.call-update
  102.8 9.3 %gather_fusion = bf16[32,512]{1,0:T(8,128)(2,1)S(1)} fusion(bf16[16064,512]{1,0:T(8,128)(2,1)} %param.25, s32[1024]{0:T(1024)S(1)} %pad_clamp_fusion), kind=kCustom, calls=%fused_computation | custom fusion | bytes 65664 | tf_op jit(solution)/shard_map/jit(_take)/gather | solution.py:138
  112.3 3.4 psum.36
  115.7 0.8 fusion.31
  116.5 0.1 fusion.25
  116.7 18.3 %psum.38 = f32[32]{0:T(128)S(1)} all-reduce(f32[32]{0:T(128)S(1)} %fusion.25), channel_id=1, replica_groups=mesh['groups'=2,'ctx'=8,'tp'=2] {'ctx'}, use_global_device_ids=true, to_apply=%region_7.8 | all-reduce | flops 32 | bytes 256 | tf_op jit(solution)/shard_map/psum | solution.py:144
  135.0 2.1 multiply_reduce_fusion
  137.2 0.4 multiply_convert_fusion
  137.6 59.6 %all-gather.14.cloned.1.call-done = bf16[4096,512]{1,0:T(8,128)(2,1)} async-done(((bf16[512,512]{1,0:T(8,128)(2,1)}), bf16[4096,512]{1,0:T(8,128)(2,1)}) %all-gather.14.cloned.1.call-update) | async-done | bytes 4194320 | tf_op jit(solution)/shard_map/all_gather | solution.py:106
  197.2 2.9 fusion.10
  200.2 0.7 copy.42
  200.9 3.4 all-to-all-start
  204.2 66.7 %all-gather.16.cloned.1.call-done = bf16[4096,512]{1,0:T(8,128)(2,1)} async-done(((bf16[512,512]{1,0:T(8,128)(2,1)}), bf16[4096,512]{1,0:T(8,128)(2,1)}) %all-gather.16.cloned.1.call-update) | async-done | bytes 4194320 | tf_op jit(solution)/shard_map/all_gather | solution.py:111
  271.0 2.9 fusion.11
  273.9 0.7 copy.43
  274.6 3.4 all-to-all-start.1
  278.1 7.3 %all-to-all-done.1 = bf16[16,8,512]{2,0,1:T(8,128)(2,1)S(1)} async-done(((bf16[16,8,512]{2,0,1:T(8,128)(2,1)}), bf16[16,8,512]{2,0,1:T(8,128)(2,1)S(1)}, u32[]{:S(2)}, u32[]{:S(2)}) %all-to-all-start.1) | async-done | bytes 131104 | tf_op jit(solution)/shard_map/all_to_all | solution.py:124
  285.4 56.9 %all-reduce.6.cloned.1.call-done = f32[32,512]{1,0:T(8,128)} async-done(((f32[32,512]{1,0:T(8,128)}), f32[32,512]{1,0:T(8,128)}) %all-reduce.6.cloned.1.call-update) | async-done | bytes 65552 | tf_op jit(solution)/shard_map/psum | solution.py:144
  342.3 1.1 fusion.53
  343.4 0.2 fusion.21
  343.7 31.4 %all-gather.2 = f32[32,32,128]{2,1,0:T(8,128)S(1)} all-gather(f32[4,32,128]{2,1,0:T(8,128)S(1)} %fusion.21), channel_id=4, replica_groups=mesh['groups'=2,'ctx'=8,'tp'=2] {'ctx'}, dimensions={0}, use_global_device_ids=true | all-gather | bytes 589824 | tf_op jit(solution)/shard_map/all_gather | solution.py:17
  375.1 0.2 fusion.28
  375.3 26.1 %all-gather.4 = f32[8,4,32]{2,1,0:T(4,128)S(1)} all-gather(f32[1,4,32]{2,1,0:T(4,128)S(1)} %bitcast.122), channel_id=3, replica_groups=mesh['groups'=2,'ctx'=8,'tp'=2] {'ctx'}, dimensions={0}, use_global_device_ids=true | all-gather | bytes 4608 | tf_op jit(solution)/shard_map/all_gather | solution.py:17
  401.4 26.1 %all-gather.3 = f32[8,4,32]{2,1,0:T(4,128)S(1)} all-gather(f32[1,4,32]{2,1,0:T(4,128)S(1)} %bitcast.121), channel_id=2, replica_groups=mesh['groups'=2,'ctx'=8,'tp'=2] {'ctx'}, dimensions={0}, use_global_device_ids=true | all-gather | bytes 4608 | tf_op jit(solution)/shard_map/all_gather | solution.py:17
  427.6 1.1 while.2
  427.7 0.1 fusion.73
  427.9 0.1 fusion.73
  428.1 0.1 fusion.73
  428.2 0.1 fusion.73
  428.4 0.1 fusion.73
  428.5 0.1 fusion.73
  428.7 0.9 fusion.33
  429.6 15.1 %all-reduce.8.cloned.1.call-done = f32[32,512]{1,0:T(8,128)} async-done(((f32[32,512]{1,0:T(8,128)}), f32[32,512]{1,0:T(8,128)}) %all-reduce.8.cloned.1.call-update) | async-done | bytes 65552 | tf_op jit(solution)/shard_map/psum | solution.py:162
  444.7 0.8 fusion.26
  445.5 0.6 reshape.129
  446.2 0.7 copy.97
  446.8 0.7 copy.98
  (62 shorter events, 1.5 us)
Async XLA Ops:
  7.2 108.5 %copy-start = (bf16[512,512]{1,0:T(8,128)(2,1)S(1)}, bf16[512,512]{1,0:T(8,128)(2,1)}, u32[]{:S(2)}) copy-start(bf16[512,512]{1,0:T(8,128)(2,1)} %param.28) | copy-start | bytes 1572868
  7.2 45.6 %all-gather.10.cloned.1.call-start = ((), (), s32[]{:S(2)}) async-start(), calls=%async_computation.2 | async-start | bytes 1179648 | tf_op jit(solution)/shard_map/all_gather | solution.py:78
  9.0 85.2 %all-gather.12.cloned.1.call-start = ((), (), s32[]{:S(2)}) async-start(), calls=%async_computation.3 | async-start | bytes 1179648 | tf_op jit(solution)/shard_map/all_gather | solution.py:79
  9.7 125.3 %all-reduce.4.cloned.1.call-start = ((), (), s32[]{:S(2)}) async-start(), calls=%async_computation.4 | async-start | bytes 4194304 | tf_op jit(solution)/shard_map/psum | solution.py:100
  96.5 2.5 copy-start.3
  101.0 1.3 copy-start.6
  101.1 1.8 copy-start.7
  101.1 15.6 %copy-start.5 = (bf16[4096]{0:T(1024)(128)(2,1)S(1)}, bf16[4096]{0:T(1024)(128)(2,1)}, u32[]{:S(2)}) copy-start(bf16[4096]{0:T(1024)(128)(2,1)} %param.22) | copy-start | bytes 24580
  101.1 34.0 %copy-start.2 = (bf16[128,4096]{1,0:T(8,128)(2,1)S(1)}, bf16[128,4096]{1,0:T(8,128)(2,1)}, u32[]{:S(2)}) copy-start(bf16[128,4096]{1,0:T(8,128)(2,1)} %param.16) | copy-start | bytes 3145732
  101.1 96.2 %all-gather.14.cloned.1.call-start = ((), (), s32[]{:S(2)}) async-start(), calls=%async_computation.5 | async-start | bytes 4718592 | tf_op jit(solution)/shard_map/all_gather | solution.py:106
  101.7 169.3 %all-gather.16.cloned.1.call-start = ((), (), s32[]{:S(2)}) async-start(), calls=%async_computation.6 | async-start | bytes 4718592 | tf_op jit(solution)/shard_map/all_gather | solution.py:111
  102.3 240.0 %all-reduce.6.cloned.1.call-start = ((), (), s32[]{:S(2)}) async-start(), calls=%async_computation.7 | async-start | bytes 131072 | tf_op jit(solution)/shard_map/psum | solution.py:144
  135.0 2.2 copy-start.1
  200.9 73.7 %all-to-all-start = ((bf16[16,8,512]{2,0,1:T(8,128)(2,1)}), bf16[16,8,512]{2,0,1:T(8,128)(2,1)S(1)}, u32[]{:S(2)}, u32[]{:S(2)}) async-start(bf16[16,8,512]{2,0,1:T(8,128)(2,1)} %copy.42), calls=%async_computation | async-start | bytes 262144 | tf_op jit(solution)/shard_map/all_to_all | solution.py:117
  274.6 10.8 %all-to-all-start.1 = ((bf16[16,8,512]{2,0,1:T(8,128)(2,1)}), bf16[16,8,512]{2,0,1:T(8,128)(2,1)S(1)}, u32[]{:S(2)}, u32[]{:S(2)}) async-start(bf16[16,8,512]{2,0,1:T(8,128)(2,1)} %copy.43), calls=%async_computation.1 | async-start | bytes 262144 | tf_op jit(solution)/shard_map/all_to_all | solution.py:124
  278.0 150.7 %copy-start.4 = (bf16[512,512]{1,0:T(8,128)(2,1)S(1)}, bf16[512,512]{1,0:T(8,128)(2,1)}, u32[]{:S(2)}) copy-start(bf16[512,512]{1,0:T(8,128)(2,1)} %param.29) | copy-start | bytes 1572868
  278.0 166.7 %all-reduce.8.cloned.1.call-start = ((), (), s32[]{:S(2)}) async-start(), calls=%async_computation.8 | async-start | bytes 131072 | tf_op jit(solution)/shard_map/psum | solution.py:162
Sparse Core Ops, SparseCore 0:
  10.6 42.1 all-gather.9
  54.9 39.2 all-gather.11
  101.2 20.0 all-reduce.3
  123.2 73.9 all-gather.13
  199.2 71.7 all-gather.15
  274.2 68.0 all-reduce.5
  429.7 14.9 all-reduce.7
where the time goes:
time: 455 us; the launch traced here: 454 us
  waiting for transfers between devices  289 us (64%)
  blocking collectives  105 us (23%)
  local copies, waits for them, and re-layouts  17.7 us (4%)
  between operations  15 us (3%)
  matrix products  14.9 us (3%)
  starting transfers between devices  7.02 us (2%)
  other arithmetic  5.36 us (1%)
    all_gather x3, blocking collectives, joined(): pieces = jax.tree.map(lambda part: lax.all_gather(part, axis), value)  83.7 us
    all_gather x1, waiting for transfers between devices, local(): lax.all_gather(cross_value_weight, 'ctx', axis=0, tiled=True)  66.7 us
    all_gather x1, waiting for transfers between devices, local(): lax.all_gather(cross_key_weight, 'ctx', axis=0, tiled=True)  59.6 us
    psum x1, waiting for transfers between devices, local(): raw, squares = lax.psum((raw_part, square_part), 'ctx')  56.9 us
    all_gather x1, waiting for transfers between devices, local(): key_rows = lax.all_gather(enc_key, 'ctx', axis=0, tiled=True)  42.3 us
    all_gather x1, waiting for transfers between devices, local(): value_rows = lax.all_gather(enc_value, 'ctx', axis=0, tiled=True)  39 us
    psum x1, blocking collectives, local(): raw, squares = lax.psum((raw_part, square_part), 'ctx')  18.3 us
    psum x1, waiting for transfers between devices, local(): out = lax.psum(out_part, 'tp')  15.1 us
  transfers between devices with their start and end apart: 9, of which 7 were waited for; matrix products, arithmetic and copies ran while one was open for 5% of the time, Pallas kernels for 0%

commit v1 on v0

--- a/solution.py
+++ b/solution.py
@@ -3,6 +3,8 @@
 import jax
 import jax.numpy as jnp
 from jax import lax
+from jax.experimental import pallas as pl
+from jax.experimental.pallas import tpu as pltpu
 from jax.sharding import PartitionSpec as P
 
 D = 4096
@@ -164,6 +166,395 @@
     return (keys_cache[None], values_cache[None], decoded)
 
 
+MESH = pl.DeviceIdType.MESH
+F32 = jnp.float32
+BF16 = jnp.bfloat16
+SUBS = 4
+CHUNKS = 2
+
+
+def pick_kernel(ids_ref, table_ref, out_ref, held, rows, sems):
+    count = out_ref.shape[0]
+    vocab_local = table_ref.shape[0]
+    base = lax.axis_index("tp") * vocab_local
+    copies = []
+    for j in range(count):
+        own = jnp.clip(ids_ref[j] - base, 0, vocab_local - 1)
+        start = pl.multiple_of(lax.div(own, 16) * 16, 16)
+        copy = pltpu.make_async_copy(table_ref.at[pl.ds(start, 16)], held.at[j], sems.at[j])
+        copy.start()
+        copies.append(copy)
+    spots = lax.broadcasted_iota(jnp.int32, held.shape[1:], 0)
+    for j in range(count):
+        copies[j].wait()
+        own = ids_ref[j] - base
+        inside = (own >= 0) & (own < vocab_local)
+        spot = jnp.where(inside, lax.rem(jnp.clip(own, 0, vocab_local - 1), 16), -1)
+        block = held[j].astype(F32)
+        rows[pl.ds(j, 1)] = jnp.sum(jnp.where(spots == spot, block, 0.0), axis=0, keepdims=True)
+    out_ref[...] = rows[...].astype(BF16)
+
+
+def fused_kernel(
+    q, k, v, ein, looked, dec_gain, wq, wo, enc_gain, wk, wv, wout, valid_enc, valid_dec,
+    keys_out, values_out, decoded_out,
+    looked_far, wo_all, qg, kg, vg, ein_all, ctx_all, raw_own, raw_out, raw_in, query_in, query_all,
+    part_k, part_v, slot_k, slot_v, square_out, square_in,
+    mixed_out, mixed_in, stats_out, stats_in, proj_out, proj_in, hidden_ref,
+    send, r_look, r_wo, r_q, r_k, r_v, r_raw, r_query, r_ein, r_ein_far, r_ctx, r_square, r_ring, r_mixed,
+    r_stats, r_proj,
+):
+    c = lax.axis_index("ctx")
+    t = lax.axis_index("tp")
+    z, y = lax.div(c, 2), lax.rem(c, 2)
+    mate, other = c + 1 - 2 * y, 1 - t
+    line = [lax.rem(z + d, 4) for d in range(1, 4)]
+    peers = [lax.rem(c + d, 8) for d in range(1, 8)]
+    rows = q.shape[0]
+    width = wq.shape[0]
+    pending = []
+
+    def put(source, target, arrival, to_ctx, to_tp):
+        copy = pltpu.make_async_remote_copy(
+            src_ref=source, dst_ref=target, send_sem=send, recv_sem=arrival,
+            device_id={"ctx": to_ctx, "tp": to_tp}, device_id_type=MESH,
+        )
+        copy.start()
+        pending.append(copy)
+
+    def got(target, arrival):
+        pltpu.make_async_remote_copy(
+            src_ref=target, dst_ref=target, send_sem=send, recv_sem=arrival,
+            device_id={"ctx": mate, "tp": t}, device_id_type=MESH,
+        ).wait_recv()
+
+    def cols(index, size):
+        return pl.ds(pl.multiple_of(index * size, size), size)
+
+    barrier = pltpu.get_barrier_semaphore()
+    for peer in peers:
+        pl.semaphore_signal(barrier, inc=1, device_id={"ctx": peer, "tp": t}, device_id_type=MESH)
+    pl.semaphore_signal(barrier, inc=1, device_id={"ctx": c, "tp": other}, device_id_type=MESH)
+    pl.semaphore_wait(barrier, len(peers) + 1)
+
+    put(looked, looked_far, r_look, c, other)
+    for far in line:
+        to = far * 2 + y
+        put(k.at[:, cols(far, HD)], kg.at[c], r_k.at[c], to, t)
+        put(v.at[:, cols(far, HD)], vg.at[c], r_v.at[c], to, t)
+        put(q.at[:, cols(far, HD)], qg.at[z], r_q.at[z], to, t)
+    put(k.at[:, cols(z, HD)], kg.at[c], r_k.at[c], mate, t)
+    put(v.at[:, cols(z, HD)], vg.at[c], r_v.at[c], mate, t)
+    put(wo, wo_all.at[cols(t, wo.shape[0])], r_wo, c, other)
+    kg[c] = k[:, cols(z, HD)]
+    vg[c] = v[:, cols(z, HD)]
+    qg[z] = q[:, cols(z, HD)]
+    wo_all[cols(t, wo.shape[0])] = wo[...]
+    ein_all[y * 4 + z] = ein[:, cols(c, width)]
+
+    got(looked_far, r_look)
+    hidden = looked[...].astype(F32) + looked_far[...].astype(F32)
+    hidden_ref[...] = hidden
+    scaled = (hidden * dec_gain[...]).astype(BF16)
+    inner = wq.shape[1]
+    raw_own[:, :inner] = jnp.dot(scaled, wq[...], preferred_element_type=F32)
+    raw_own[:, inner:] = jnp.broadcast_to(
+        jnp.sum(hidden * hidden, axis=-1, keepdims=True), (hidden.shape[0], 128)
+    )
+    share = hidden.shape[0] // 8
+    for j in range(8):
+        raw_out[j] = raw_own[j * share : (j + 1) * share, :]
+    for peer in peers:
+        put(raw_out.at[peer], raw_in.at[c], r_raw.at[c], peer, t)
+    raw_in[c] = raw_out[c]
+
+    for far in line:
+        source = far * 2 + y
+        got(kg.at[source], r_k.at[source])
+        put(kg.at[source], kg.at[source], r_k.at[source], mate, t)
+        got(vg.at[source], r_v.at[source])
+        put(vg.at[source], vg.at[source], r_v.at[source], mate, t)
+    half = rows // 2
+    for peer in peers:
+        put(
+            ein.at[cols(t, half), cols(peer, width)],
+            ein_all.at[y * 4 + z, cols(t, half)],
+            r_ein.at[c], peer, t,
+        )
+    for far in line:
+        got(qg.at[far], r_q.at[far])
+    for far in range(4):
+        source = far * 2 + 1 - y
+        got(kg.at[source], r_k.at[source])
+        got(vg.at[source], r_v.at[source])
+
+    def block(core, head, side, chunk):
+        size = 4 * rows // CHUNKS
+        place = ctx_all.at[side, pl.ds(chunk * size, size), cols(core * 4 + head, HD)]
+        return place, r_ctx.at[(core * 4 + head) * 2 + side, chunk]
+
+    every_key = kg[...].reshape(8 * rows, HD)
+    every_value = vg[...].reshape(8 * rows, HD)
+    valid = valid_enc[...] > 0.0
+    for chunk in range(CHUNKS):
+        some = 4 // CHUNKS
+        queries = qg[chunk * some : (chunk + 1) * some].reshape(some * rows, HD)
+        scores = lax.dot_general(
+            queries, every_key, (((1,), (1,)), ((), ())), preferred_element_type=F32
+        ) * (HD ** (-0.5))
+        scores = jnp.where(valid, scores, FLOOR)
+        top = jnp.max(scores, axis=-1, keepdims=True)
+        probs = jnp.where(valid, jnp.exp(scores - top), 0.0)
+        total = jnp.sum(probs, axis=-1, keepdims=True)
+        mixed = jnp.dot(probs.astype(BF16), every_value, preferred_element_type=F32)
+        ctx_all[y, pl.ds(chunk * some * rows, some * rows), cols(t * 4 + z, HD)] = (mixed / total).astype(BF16)
+        place, arrival = block(t, z, y, chunk)
+        for far in line:
+            put(place, place, arrival, far * 2 + y, t)
+        put(place, place, arrival, mate, t)
+        put(place, place, arrival, c, other)
+
+    for peer in peers:
+        got(raw_in.at[peer], r_raw.at[peer])
+    raw = raw_in[0]
+    for j in range(1, 8):
+        raw = raw + raw_in[j]
+    factor = lax.rsqrt(raw[:, inner : inner + 1] / D + EPSILON)
+    query_in[c] = (raw[:, :inner] * factor * HD ** (-0.5)).astype(BF16).astype(F32)
+    for peer in peers:
+        put(query_in.at[c], query_in.at[c], r_query.at[c], peer, t)
+
+    for peer in peers:
+        place = ein_all.at[lax.rem(peer, 2) * 4 + lax.div(peer, 2), cols(t, half)]
+        got(place, r_ein.at[peer])
+        put(place, place, r_ein_far.at[peer], c, other)
+    for chunk in range(CHUNKS):
+        for far in line:
+            place, arrival = block(t, far, y, chunk)
+            got(place, arrival)
+            put(place, place, arrival, mate, t)
+            put(place, place, arrival, c, other)
+    for chunk in range(CHUNKS):
+        for far in range(4):
+            place, arrival = block(t, far, 1 - y, chunk)
+            got(place, arrival)
+            put(place, place, arrival, c, other)
+    got(wo_all.at[cols(other, wo.shape[0])], r_wo)
+    for peer in peers:
+        place = ein_all.at[lax.rem(peer, 2) * 4 + lax.div(peer, 2), cols(other, half)]
+        got(place, r_ein_far.at[peer])
+    for chunk in range(CHUNKS):
+        for side in range(2):
+            for far in range(4):
+                place, arrival = block(other, far, side, chunk)
+                got(place, arrival)
+
+    each = rows // 8
+    spot_row = lax.broadcasted_iota(jnp.int32, (rows, rows), 0)
+    spot_col = lax.broadcasted_iota(jnp.int32, (rows, rows), 1)
+    squares = jnp.zeros((8, rows), F32)
+    for side in range(2):
+        for far in range(4):
+            source = far * 2 + side
+            resid = jnp.dot(
+                ctx_all[side, far * rows : (far + 1) * rows, :], wo_all[...], preferred_element_type=F32
+            ) + ein_all[side * 4 + far].astype(F32)
+            spread = jnp.where(
+                spot_col == source * each + lax.rem(spot_row, each),
+                jnp.sum(resid * resid, axis=-1, keepdims=True),
+                0.0,
+            )
+            squares = squares + jnp.sum(spread.reshape(8, each, rows), axis=1)
+            gained = (resid * enc_gain[...]).astype(BF16)
+            term_k = jnp.dot(gained, wk[...], preferred_element_type=F32).astype(BF16)
+            term_v = jnp.dot(gained, wv[...], preferred_element_type=F32).astype(BF16)
+            for r in range(8):
+                part_k[r, source * each : (source + 1) * each, :] = term_k[r * each : (r + 1) * each]
+                part_v[r, source * each : (source + 1) * each, :] = term_v[r * each : (r + 1) * each]
+    for r in range(8):
+        square_out[r] = squares[r : r + 1]
+
+    def at_ring(place):
+        place = lax.rem(place + 16, 8)
+        return jnp.where(place < 4, place * 2, (7 - place) * 2 + 1)
+
+    spot = z + y * (7 - 2 * z)
+    piece = rows // SUBS
+    ways = ((part_k, slot_k, 1), (part_v, slot_v, -1))
+    for sub in range(SUBS):
+        lines = pl.ds(sub * piece, piece)
+        for way, (part, slot, step) in enumerate(ways):
+            put(
+                part.at[at_ring(spot - step), lines], slot.at[0, lines],
+                r_ring.at[way, 0, sub], at_ring(spot + step), t,
+            )
+    for peer in peers:
+        put(square_out.at[peer], square_in.at[c], r_square.at[c], peer, t)
+    square_in[c] = square_out[c]
+    for peer in peers:
+        got(query_in.at[peer], r_query.at[peer])
+    for j in range(8):
+        query_all[j * share : (j + 1) * share, :] = query_in[j]
+    for peer in peers:
+        got(square_in.at[peer], r_square.at[peer])
+    square = square_in[0]
+    for j in range(1, 8):
+        square = square + square_in[j]
+    column = jnp.sum(jnp.where(spot_row == spot_col, square, 0.0), axis=-1, keepdims=True)
+    scale = lax.rsqrt(column / D + EPSILON)
+
+    for hop in range(7):
+        for sub in range(SUBS):
+            lines = pl.ds(sub * piece, piece)
+            for way, (part, slot, step) in enumerate(ways):
+                got(slot.at[hop, lines], r_ring.at[way, hop, sub])
+                here = part[at_ring(spot - step * (hop + 2)), lines].astype(F32)
+                running = slot[hop, lines].astype(F32) + here
+                if hop < 6:
+                    slot[hop, lines] = running.astype(BF16)
+                    put(
+                        slot.at[hop, lines], slot.at[hop + 1, lines],
+                        r_ring.at[way, hop + 1, sub], at_ring(spot + step), t,
+                    )
+                else:
+                    out = keys_out if way == 0 else values_out
+                    out[lines] = (running * scale[sub * piece : (sub + 1) * piece]).astype(BF16)
+
+    own_valid = valid_dec[...] > 0.0
+    lanes = lax.broadcasted_iota(jnp.int32, stats_out.shape, 1)
+    stats = jnp.zeros(stats_out.shape, F32)
+    heads = inner // HD
+    for head in range(heads):
+        part = slice(head * HD, (head + 1) * HD)
+        scores = lax.dot_general(
+            query_all[:, part].astype(BF16), keys_out[:, part], (((1,), (1,)), ((), ())),
+            preferred_element_type=F32,
+        )
+        scores = jnp.where(own_valid, scores, FLOOR)
+        top = jnp.max(scores, axis=-1, keepdims=True)
+        probs = jnp.where(own_valid, jnp.exp(scores - top), 0.0)
+        stats = jnp.where(lanes == head, top, stats)
+        stats = jnp.where(lanes == heads + head, jnp.sum(probs, axis=-1, keepdims=True), stats)
+        mixed_out[:, part] = jnp.dot(
+            probs.astype(BF16), values_out[:, part], preferred_element_type=F32
+        ).astype(BF16)
+    stats_out[...] = stats
+    for peer in peers:
+        put(stats_out, stats_in.at[c], r_stats.at[c], peer, t)
+        put(mixed_out, mixed_in.at[c], r_mixed.at[c], peer, t)
+    stats_in[c] = stats_out[...]
+    mixed_in[c] = mixed_out[...]
+    for peer in peers:
+        got(stats_in.at[peer], r_stats.at[peer])
+        got(mixed_in.at[peer], r_mixed.at[peer])
+    proj = jnp.zeros(proj_out.shape, F32)
+    for head in range(heads):
+        part = slice(head * HD, (head + 1) * HD)
+        tops = [stats_in[j][:, head : head + 1] for j in range(8)]
+        top = tops[0]
+        for j in range(1, 8):
+            top = jnp.maximum(top, tops[j])
+        total = jnp.zeros_like(top)
+        mixed = jnp.zeros((top.shape[0], HD), F32)
+        for j in range(8):
+            weight = jnp.exp(tops[j] - top)
+            total = total + stats_in[j][:, heads + head : heads + head + 1] * weight
+            mixed = mixed + mixed_in[j][:, part].astype(F32) * weight
+        proj = proj + jnp.dot((mixed / total).astype(BF16), wout[part, :], preferred_element_type=F32)
+    proj_out[...] = proj
+    put(proj_out, proj_in, r_proj, c, other)
+    got(proj_in, r_proj)
+    decoded_out[...] = (proj_out[...] + proj_in[...] + hidden_ref[...]).astype(BF16)
+    for copy in pending:
+        copy.wait_send()
+
+
+def local_fused(
+    enc_input, enc_query, enc_key, enc_value, seq_length, attn_out_weight, enc_gain, cross_key_weight,
+    cross_value_weight, embed_table, dec_ids, dec_gain, cross_query_weight, cross_out_weight,
+):
+    rows, inner = enc_query.shape
+    width = cross_query_weight.shape[0]
+    c = lax.axis_index("ctx")
+    tokens = dec_ids.size
+    whole = pl.BlockSpec(memory_space=pltpu.VMEM)
+    looked = pl.pallas_call(
+        pick_kernel,
+        out_shape=jax.ShapeDtypeStruct((tokens, width), BF16),
+        in_specs=[pl.BlockSpec(memory_space=pltpu.SMEM), pl.BlockSpec(memory_space=pl.ANY)],
+        out_specs=whole,
+        scratch_shapes=[
+            pltpu.VMEM((tokens, 16, width), BF16),
+            pltpu.VMEM((tokens, width), F32),
+            pltpu.SemaphoreType.DMA((tokens,)),
+        ],
+    )(dec_ids.reshape(-1), embed_table)
+    order = jnp.arange(rows, dtype=jnp.int32)
+    wanted = (order % (rows // 8)) * 8 + order // (rows // 8)
+    turn = (wanted[:, None] == order[None, :]).astype(BF16)
+    query = jnp.dot(turn, enc_query, preferred_element_type=F32).astype(BF16)
+    ein = jnp.dot(turn, enc_input, preferred_element_type=F32).astype(BF16)
+    wo = lax.dynamic_slice_in_dim(attn_out_weight, c * width, width, 1)
+    gain = lax.dynamic_slice_in_dim(enc_gain, c * width, width, 0).astype(F32)[None]
+    limit = seq_length[0]
+    valid_enc = (jnp.arange(8 * rows, dtype=jnp.int32) < limit).astype(F32)[None]
+    valid_dec = (order * 8 + c < limit).astype(F32)[None]
+    dma = pltpu.SemaphoreType.DMA
+    share = tokens // 8
+    keys, values, decoded = pl.pallas_call(
+        fused_kernel,
+        out_shape=(
+            jax.ShapeDtypeStruct((rows, inner), BF16),
+            jax.ShapeDtypeStruct((rows, inner), BF16),
+            jax.ShapeDtypeStruct((tokens, width), BF16),
+        ),
+        in_specs=[whole] * 14,
+        out_specs=(whole, whole, whole),
+        scratch_shapes=[
+            pltpu.VMEM((tokens, width), BF16),
+            pltpu.VMEM((2 * inner, width), BF16),
+            pltpu.VMEM((4, rows, HD), BF16),
+            pltpu.VMEM((8, rows, HD), BF16),
+            pltpu.VMEM((8, rows, HD), BF16),
+            pltpu.VMEM((8, rows, width), BF16),
+            pltpu.VMEM((2, 4 * rows, 2 * inner), BF16),
+            pltpu.VMEM((tokens, inner + 128), F32),
+            pltpu.VMEM((8, share, inner + 128), F32),
+            pltpu.VMEM((8, share, inner + 128), F32),
+            pltpu.VMEM((8, share, inner), F32),
+            pltpu.VMEM((tokens, inner), F32),
+            pltpu.VMEM((8, rows, inner), BF16),
+            pltpu.VMEM((8, rows, inner), BF16),
+            pltpu.VMEM((7, rows, inner), BF16),
+            pltpu.VMEM((7, rows, inner), BF16),
+            pltpu.VMEM((8, 1, rows), F32),
+            pltpu.VMEM((8, 1, rows), F32),
+            pltpu.VMEM((tokens, inner), BF16),
+            pltpu.VMEM((8, tokens, inner), BF16),
+            pltpu.VMEM((tokens, 128), F32),
+            pltpu.VMEM((8, tokens, 128), F32),
+            pltpu.VMEM((tokens, width), F32),
+            pltpu.VMEM((tokens, width), F32),
+            pltpu.VMEM((tokens, width), F32),
+            dma, dma, dma, dma((4,)), dma((8,)), dma((8,)), dma((8,)), dma((8,)), dma((8,)), dma((8,)),
+            dma((16, CHUNKS)), dma((8,)), dma((2, 7, SUBS)), dma((8,)), dma((8,)), dma,
+        ],
+        compiler_params=pltpu.CompilerParams(
+            collective_id=0, has_side_effects=True, vmem_limit_bytes=60 * 1024 * 1024
+        ),
+    )(
+        query, enc_key, enc_value, ein, looked, dec_gain.astype(F32)[None], cross_query_weight, wo, gain,
+        cross_key_weight, cross_value_weight, cross_out_weight, valid_enc, valid_dec,
+    )
+    return keys[None], values[None], decoded.reshape(dec_ids.shape[0], 2, width)
+
+
+def chosen(*arrays):
+    rows, inner = arrays[1].shape
+    fits = lax.axis_size("ctx") == 8 and lax.axis_size("tp") == 2 and (rows, inner) == (128, 4 * HD)
+    return (local_fused if fits else local)(*arrays)
+
+
 def solution(mesh):
     placed = (
         P(("groups", "ctx"), None),
@@ -182,7 +573,7 @@
         P("tp", "ctx"),
     )
     return jax.shard_map(
-        local,
+        chosen,
         mesh=mesh,
         in_specs=placed,
         out_specs=(

time: 455 us -> 111 us (0.24)
  waiting for transfers between devices: 289 us -> 0 us
  blocking collectives: 105 us -> 0 us
  Pallas kernels: 0 us -> 94.5 us
  between operations: 15 us -> 1.41 us
  matrix products: 14.9 us -> 2.34 us
  local copies, waits for them, and re-layouts: 17.7 us -> 7.77 us
  starting transfers between devices: 7.02 us -> 0 us
    all_gather x4 -> x0, waiting for transfers between devices: 208 us -> none  [the longest x1 66.7 us: local(): lax.all_gather(cross_value_weight, 'ctx', axis=0, tiled=True)]
    pallas_call x0 -> x2, Pallas kernels: none -> 94.5 us  [the longest x1 91.4 us: local_fused(): pl.pallas_call(fused_kernel, out_shape=(jax.ShapeDtypeStruct((rows, inner...]
    all_gather x3 -> x0, blocking collectives: 83.7 us -> none  [joined(): pieces = jax.tree.map(lambda part: lax.all_gather(part, axis), value)]
    psum x3 -> x0, waiting for transfers between devices: 72 us -> none  [the longest x1 56.9 us: local(): raw, squares = lax.psum((raw_part, square_part), 'ctx')]
    psum x2 -> x0, blocking collectives: 21.7 us -> none  [the longest x1 18.3 us: local(): raw, squares = lax.psum((raw_part, square_part), 'ctx')]
    dot_general x9 -> x2, matrix products: 14.9 us -> 2.34 us  [the longest x1 1.45 us: local_fused(): ein = jnp.dot(turn, enc_input, preferred_element_type=F32).astype(BF16)]
    gather x1 -> x0, local copies, waits for them, and re-layouts: 9.32 us -> none  [local(): jnp.take(embed_table, jnp.clip(flat_ids, 0, vocab_local - 1), axis=0)]
    all_to_all x2 -> x0, waiting for transfers between devices: 7.26 us -> none  [the longest x1 7.26 us: local(): lax.all_to_all(value_rows.reshape(slots, ctx_count, inner_local), 'ctx',...]
  transfers between devices with their start and end apart: 9 -> 0, of which waited for: 7 -> 0; matrix products, arithmetic and copies ran while one was open for 5% -> 0% of each run, Pallas kernels for 0% -> 0%
where the time goes in v1:
time: 111 us; the launch traced here: 110 us
  Pallas kernels  94.5 us (85%)
  local copies, waits for them, and re-layouts  7.77 us (7%)
  other arithmetic  3.79 us (3%)
  matrix products  2.34 us (2%)
  between operations  1.41 us (1%)
    pallas_call x1, Pallas kernels, local_fused(): pl.pallas_call(fused_kernel, out_shape=(jax.ShapeDtypeStruct((rows, inner...  91.4 us
    unnamed x7, local copies, waits for them, and re-layouts  3.9 us
    pallas_call x1, Pallas kernels, local_fused(): pl.pallas_call(pick_kernel, out_shape=jax.ShapeDtypeStruct((tokens, width...  3.11 us

profile of v1, /device:TPU:0, one launch (start us, length us, event | category | flops | bytes accessed | tf_op | source)
XLA Modules:
  0.0 109.8 jit_solution(12495985653927035708)
XLA Ops:
  0.6 0.0 copy-start
  1.4 0.6 compare_convert_fusion.1.valid_dec
  2.0 1.3 %dynamic-slice_convert_fusion = f32[512]{0:T(512)} fusion(bf16[4096]{0:T(1024)(128)(2,1)} %param.20, s32[]{:T(128)S(6)} %select_n.30), kind=kLoop, calls=%fused_computation.9 | loop fusion | flops 512 | bytes 3076 | tf_op jit(solution)/shard_map/broadcast_in_dim | solution.py:498
  3.3 1.3 %broadcast_in_dim.26 = f32[512]{0:T(512)} convert(bf16[512]{0:T(512)(128)(2,1)} %param.25) | non-fusion elementwise | flops 512 | bytes 3072 | tf_op jit(solution)/shard_map/broadcast_in_dim | solution.py:546
  4.6 0.6 compare_convert_fusion.valid_enc
  5.2 0.8 copy.18
  5.9 0.6 reshape.60.ids_ref
  6.5 0.0 copy-start.1
  6.5 3.1 %shard_map.157.looked = bf16[32,512]{1,0:T(8,128)(2,1)} custom-call(s32[32]{0:T(128)} %reshape.60.ids_ref, bf16[16064,512]{1,0:T(8,128)(2,1)} %table_ref.1), custom_call_target="tpu_custom_call" | custom-call | tf_op jit(solution)/shard_map/pallas_call | solution.py:481
  9.6 0.0 copy-done.1
  9.7 0.9 convolution_convert_fusion.1.q
  10.5 1.9 %constant_dynamic-slice_fusion.wo = bf16[512,512]{1,0:T(8,128)(2,1)} fusion(bf16[512,4096]{1,0:T(8,128)(2,1)} %param.19, s32[]{:T(128)S(6)} %select_n.30), kind=kLoop, calls=%fused_computation.15 | loop fusion | bytes 1048580 | tf_op jit(solution)/shard_map/dynamic_slice | solution.py:497
  12.4 0.0 copy-done
  12.4 1.5 %convolution_convert_fusion.ein = bf16[128,4096]{1,0:T(8,128)(2,1)} fusion(bf16[128,4096]{1,0:T(8,128)(2,1)S(1)} %copy-done, s32[128]{0:T(128)S(1)} %fusion.3), kind=kOutput, calls=%fused_computation | convolution fusion | flops 134758400 | bytes 2097664 | tf_op jit(solution)/shard_map/dot_general | solution.py:496
  13.9 91.4 %shard_map.158 = (bf16[128,512]{1,0:T(8,128)(2,1)}, bf16[128,512]{1,0:T(8,128)(2,1)}, bf16[32,512]{1,0:T(8,128)(2,1)}) custom-call(bf16[128,512]{1,0:T(8,128)(2,1)} %convolution_convert_fusion.1.q, bf16[128,512]{1,0:T(8,128)(2,1)} %k.1, bf16[128,512]{1,0:T(8,128)(2,1)} %v.1, bf16[128,4096]{1,0:T(8,128)(2,1)} %convolution_convert_fusion.ein, ...), custom_call_target="tpu_custom_call" | custom-call | tf_op jit(solution)/shard_map/pallas_call | solution.py:504
  105.3 1.4 %reshape.61 = bf16[16,2,512]{2,1,0:T(2,128)(2,1)} reshape(bf16[32,512]{1,0:T(8,128)(2,1)} %get-tuple-element.8) | data formatting | bytes 65536 | tf_op jit(solution)/shard_map/reshape | solution.py:549
  106.7 1.6 %copy.22 = bf16[1,128,512]{2,1,0:T(8,128)(2,1)} copy(bf16[1,128,512]{2,1,0:T(8,128)(2,1)} %bitcast.10) | data formatting | bytes 262144
  108.2 1.6 %copy.23 = bf16[1,128,512]{2,1,0:T(8,128)(2,1)} copy(bf16[1,128,512]{2,1,0:T(8,128)(2,1)} %bitcast.9) | data formatting | bytes 262144
  (1 shorter events, 0.0 us)
Async XLA Ops:
  0.6 11.8 %copy-start = (bf16[128,4096]{1,0:T(8,128)(2,1)S(1)}, bf16[128,4096]{1,0:T(8,128)(2,1)}, u32[]{:S(2)}) copy-start(bf16[128,4096]{1,0:T(8,128)(2,1)} %param.14) | copy-start | bytes 3145732
  6.5 3.1 %copy-start.1 = (bf16[128,512]{1,0:T(8,128)(2,1)S(1)}, bf16[128,512]{1,0:T(8,128)(2,1)}, u32[]{:S(2)}) copy-start(bf16[128,512]{1,0:T(8,128)(2,1)} %param.15) | copy-start | bytes 393220

commit v2 on v1

--- a/solution.py
+++ b/solution.py
@@ -173,7 +173,7 @@
 CHUNKS = 2
 
 
-def pick_kernel(ids_ref, table_ref, out_ref, held, rows, sems):
+def pick_kernel(ids_ref, length_ref, table_ref, out_ref, enc_mask, dec_mask, held, rows, sems):
     count = out_ref.shape[0]
     vocab_local = table_ref.shape[0]
     base = lax.axis_index("tp") * vocab_local
@@ -184,6 +184,10 @@
         copy = pltpu.make_async_copy(table_ref.at[pl.ds(start, 16)], held.at[j], sems.at[j])
         copy.start()
         copies.append(copy)
+    limit = length_ref[0]
+    enc_mask[...] = (lax.broadcasted_iota(jnp.int32, enc_mask.shape, 1) < limit).astype(F32)
+    places = lax.broadcasted_iota(jnp.int32, dec_mask.shape, 1) * 8 + lax.axis_index("ctx")
+    dec_mask[...] = (places < limit).astype(F32)
     spots = lax.broadcasted_iota(jnp.int32, held.shape[1:], 0)
     for j in range(count):
         copies[j].wait()
@@ -195,14 +199,21 @@
     out_ref[...] = rows[...].astype(BF16)
 
 
+def hand_kernel(keys_ref, values_ref, decoded_ref, keys_out, values_out, decoded_out):
+    keys_out[0] = keys_ref[...]
+    values_out[0] = values_ref[...]
+    for i in range(decoded_out.shape[0]):
+        decoded_out[i] = decoded_ref[2 * i : 2 * i + 2].astype(BF16)
+
+
 def fused_kernel(
-    q, k, v, ein, looked, dec_gain, wq, wo, enc_gain, wk, wv, wout, valid_enc, valid_dec,
+    q, k, v, ein, looked, dec_gain, wq, wo, enc_gain, wk_far, wv_far, wout_far, valid_enc, valid_dec,
     keys_out, values_out, decoded_out,
     looked_far, wo_all, qg, kg, vg, ein_all, ctx_all, raw_own, raw_out, raw_in, query_in, query_all,
-    part_k, part_v, slot_k, slot_v, square_out, square_in,
+    wk, wv, wout, gained_all, part_k, part_v, slot_k, slot_v, square_out, square_in,
     mixed_out, mixed_in, stats_out, stats_in, proj_out, proj_in, hidden_ref,
     send, r_look, r_wo, r_q, r_k, r_v, r_raw, r_query, r_ein, r_ein_far, r_ctx, r_square, r_ring, r_mixed,
-    r_stats, r_proj,
+    r_stats, r_proj, fetched,
 ):
     c = lax.axis_index("ctx")
     t = lax.axis_index("tp")
@@ -228,6 +239,11 @@
             device_id={"ctx": mate, "tp": t}, device_id_type=MESH,
         ).wait_recv()
 
+    def fetch(source, target, arrival):
+        copy = pltpu.make_async_copy(source, target, arrival)
+        copy.start()
+        return copy
+
     def cols(index, size):
         return pl.ds(pl.multiple_of(index * size, size), size)
 
@@ -245,17 +261,22 @@
         put(q.at[:, cols(far, HD)], qg.at[z], r_q.at[z], to, t)
     put(k.at[:, cols(z, HD)], kg.at[c], r_k.at[c], mate, t)
     put(v.at[:, cols(z, HD)], vg.at[c], r_v.at[c], mate, t)
-    put(wo, wo_all.at[cols(t, wo.shape[0])], r_wo, c, other)
+    put(wo.at[:, cols(c, width)], wo_all.at[cols(t, wo.shape[0])], r_wo, c, other)
+    fetches = [
+        fetch(wo.at[:, cols(c, width)], wo_all.at[cols(t, wo.shape[0])], fetched.at[0]),
+        fetch(ein.at[:, cols(c, width)], ein_all.at[y * 4 + z], fetched.at[1]),
+        fetch(wk_far, wk, fetched.at[2]),
+        fetch(wv_far, wv, fetched.at[3]),
+        fetch(wout_far, wout, fetched.at[4]),
+    ]
     kg[c] = k[:, cols(z, HD)]
     vg[c] = v[:, cols(z, HD)]
     qg[z] = q[:, cols(z, HD)]
-    wo_all[cols(t, wo.shape[0])] = wo[...]
-    ein_all[y * 4 + z] = ein[:, cols(c, width)]
 
     got(looked_far, r_look)
     hidden = looked[...].astype(F32) + looked_far[...].astype(F32)
     hidden_ref[...] = hidden
-    scaled = (hidden * dec_gain[...]).astype(BF16)
+    scaled = (hidden * dec_gain[...].astype(F32)).astype(BF16)
     inner = wq.shape[1]
     raw_own[:, :inner] = jnp.dot(scaled, wq[...], preferred_element_type=F32)
     raw_own[:, inner:] = jnp.broadcast_to(
@@ -343,34 +364,37 @@
     for peer in peers:
         place = ein_all.at[lax.rem(peer, 2) * 4 + lax.div(peer, 2), cols(other, half)]
         got(place, r_ein_far.at[peer])
+    for copy in fetches:
+        copy.wait()
+
+    each = rows // 8
+    spot_row = lax.broadcasted_iota(jnp.int32, (rows, rows), 0)
+    spot_col = lax.broadcasted_iota(jnp.int32, (rows, rows), 1)
+    turn = (spot_col == lax.rem(spot_row, each) * 8 + lax.div(spot_row, each)).astype(BF16)
+    picked = lax.broadcasted_iota(jnp.int32, enc_gain.shape, 0) == c
+    gain = jnp.sum(jnp.where(picked, enc_gain[...].astype(F32), 0.0), axis=0, keepdims=True)
+    squares = jnp.zeros((8, rows), F32)
     for chunk in range(CHUNKS):
         for side in range(2):
             for far in range(4):
                 place, arrival = block(other, far, side, chunk)
                 got(place, arrival)
-
-    each = rows // 8
-    spot_row = lax.broadcasted_iota(jnp.int32, (rows, rows), 0)
-    spot_col = lax.broadcasted_iota(jnp.int32, (rows, rows), 1)
-    squares = jnp.zeros((8, rows), F32)
-    for side in range(2):
-        for far in range(4):
-            source = far * 2 + side
-            resid = jnp.dot(
-                ctx_all[side, far * rows : (far + 1) * rows, :], wo_all[...], preferred_element_type=F32
-            ) + ein_all[side * 4 + far].astype(F32)
-            spread = jnp.where(
-                spot_col == source * each + lax.rem(spot_row, each),
-                jnp.sum(resid * resid, axis=-1, keepdims=True),
-                0.0,
-            )
-            squares = squares + jnp.sum(spread.reshape(8, each, rows), axis=1)
-            gained = (resid * enc_gain[...]).astype(BF16)
-            term_k = jnp.dot(gained, wk[...], preferred_element_type=F32).astype(BF16)
-            term_v = jnp.dot(gained, wv[...], preferred_element_type=F32).astype(BF16)
-            for r in range(8):
-                part_k[r, source * each : (source + 1) * each, :] = term_k[r * each : (r + 1) * each]
-                part_v[r, source * each : (source + 1) * each, :] = term_v[r * each : (r + 1) * each]
+        for side in range(2):
+            for far in range(chunk * 4 // CHUNKS, (chunk + 1) * 4 // CHUNKS):
+                source = far * 2 + side
+                resid = jnp.dot(
+                    ctx_all[side, far * rows : (far + 1) * rows, :], wo_all[...], preferred_element_type=F32
+                ) + ein_all[side * 4 + far].astype(F32)
+                spread = jnp.where(
+                    spot_col == source * each + lax.div(spot_row, 8),
+                    jnp.sum(resid * resid, axis=-1, keepdims=True),
+                    0.0,
+                )
+                squares = squares + jnp.sum(spread.reshape(each, 8, rows), axis=0)
+                gained = (resid * gain).astype(BF16)
+                moved = jnp.dot(turn, gained, preferred_element_type=F32).astype(BF16)
+                for r in range(8):
+                    gained_all[r, source * each : (source + 1) * each, :] = moved[r * each : (r + 1) * each]
     for r in range(8):
         square_out[r] = squares[r : r + 1]
 
@@ -380,12 +404,19 @@
 
     spot = z + y * (7 - 2 * z)
     piece = rows // SUBS
-    ways = ((part_k, slot_k, 1), (part_v, slot_v, -1))
+    ways = ((part_k, slot_k, 1, wk), (part_v, slot_v, -1, wv))
+
+    def term(hop):
+        for part, slot, step, weight in ways:
+            own = gained_all[at_ring(spot - step * (hop + 1))]
+            part[hop] = jnp.dot(own, weight[...], preferred_element_type=F32).astype(BF16)
+
+    term(0)
     for sub in range(SUBS):
         lines = pl.ds(sub * piece, piece)
-        for way, (part, slot, step) in enumerate(ways):
+        for way, (part, slot, step, weight) in enumerate(ways):
             put(
-                part.at[at_ring(spot - step), lines], slot.at[0, lines],
+                part.at[0, lines], slot.at[0, lines],
                 r_ring.at[way, 0, sub], at_ring(spot + step), t,
             )
     for peer in peers:
@@ -403,12 +434,13 @@
     column = jnp.sum(jnp.where(spot_row == spot_col, square, 0.0), axis=-1, keepdims=True)
     scale = lax.rsqrt(column / D + EPSILON)
 
+    term(1)
     for hop in range(7):
         for sub in range(SUBS):
             lines = pl.ds(sub * piece, piece)
-            for way, (part, slot, step) in enumerate(ways):
+            for way, (part, slot, step, weight) in enumerate(ways):
                 got(slot.at[hop, lines], r_ring.at[way, hop, sub])
-                here = part[at_ring(spot - step * (hop + 2)), lines].astype(F32)
+                here = part[hop + 1, lines].astype(F32)
                 running = slot[hop, lines].astype(F32) + here
                 if hop < 6:
                     slot[hop, lines] = running.astype(BF16)
@@ -419,6 +451,8 @@
                 else:
                     out = keys_out if way == 0 else values_out
                     out[lines] = (running * scale[sub * piece : (sub + 1) * piece]).astype(BF16)
+        if hop < 6:
+            term(hop + 2)
 
     own_valid = valid_dec[...] > 0.0
     lanes = lax.broadcasted_iota(jnp.int32, stats_out.shape, 1)
@@ -464,7 +498,7 @@
     proj_out[...] = proj
     put(proj_out, proj_in, r_proj, c, other)
     got(proj_in, r_proj)
-    decoded_out[...] = (proj_out[...] + proj_in[...] + hidden_ref[...]).astype(BF16)
+    decoded_out[...] = proj_out[...] + proj_in[...] + hidden_ref[...]
     for copy in pending:
         copy.wait_send()
 
@@ -475,30 +509,25 @@
 ):
     rows, inner = enc_query.shape
     width = cross_query_weight.shape[0]
-    c = lax.axis_index("ctx")
     tokens = dec_ids.size
     whole = pl.BlockSpec(memory_space=pltpu.VMEM)
-    looked = pl.pallas_call(
+    scalars = pl.BlockSpec(memory_space=pltpu.SMEM)
+    anywhere = pl.BlockSpec(memory_space=pl.ANY)
+    looked, valid_enc, valid_dec = pl.pallas_call(
         pick_kernel,
-        out_shape=jax.ShapeDtypeStruct((tokens, width), BF16),
-        in_specs=[pl.BlockSpec(memory_space=pltpu.SMEM), pl.BlockSpec(memory_space=pl.ANY)],
-        out_specs=whole,
+        out_shape=(
+            jax.ShapeDtypeStruct((tokens, width), BF16),
+            jax.ShapeDtypeStruct((1, 8 * rows), F32),
+            jax.ShapeDtypeStruct((1, rows), F32),
+        ),
+        in_specs=[scalars, scalars, anywhere],
+        out_specs=(whole, whole, whole),
         scratch_shapes=[
             pltpu.VMEM((tokens, 16, width), BF16),
             pltpu.VMEM((tokens, width), F32),
             pltpu.SemaphoreType.DMA((tokens,)),
         ],
-    )(dec_ids.reshape(-1), embed_table)
-    order = jnp.arange(rows, dtype=jnp.int32)
-    wanted = (order % (rows // 8)) * 8 + order // (rows // 8)
-    turn = (wanted[:, None] == order[None, :]).astype(BF16)
-    query = jnp.dot(turn, enc_query, preferred_element_type=F32).astype(BF16)
-    ein = jnp.dot(turn, enc_input, preferred_element_type=F32).astype(BF16)
-    wo = lax.dynamic_slice_in_dim(attn_out_weight, c * width, width, 1)
-    gain = lax.dynamic_slice_in_dim(enc_gain, c * width, width, 0).astype(F32)[None]
-    limit = seq_length[0]
-    valid_enc = (jnp.arange(8 * rows, dtype=jnp.int32) < limit).astype(F32)[None]
-    valid_dec = (order * 8 + c < limit).astype(F32)[None]
+    )(dec_ids.reshape(-1), seq_length, embed_table)
     dma = pltpu.SemaphoreType.DMA
     share = tokens // 8
     keys, values, decoded = pl.pallas_call(
@@ -506,9 +535,12 @@
         out_shape=(
             jax.ShapeDtypeStruct((rows, inner), BF16),
             jax.ShapeDtypeStruct((rows, inner), BF16),
-            jax.ShapeDtypeStruct((tokens, width), BF16),
+            jax.ShapeDtypeStruct((tokens, width), F32),
         ),
-        in_specs=[whole] * 14,
+        in_specs=[
+            whole, whole, whole, anywhere, whole, whole, whole, anywhere, whole, anywhere, anywhere, anywhere,
+            whole, whole,
+        ],
         out_specs=(whole, whole, whole),
         scratch_shapes=[
             pltpu.VMEM((tokens, width), BF16),
@@ -523,6 +555,10 @@
             pltpu.VMEM((8, share, inner + 128), F32),
             pltpu.VMEM((8, share, inner), F32),
             pltpu.VMEM((tokens, inner), F32),
+            pltpu.VMEM((width, inner), BF16),
+            pltpu.VMEM((width, inner), BF16),
+            pltpu.VMEM((inner, width), BF16),
+            pltpu.VMEM((8, rows, width), BF16),
             pltpu.VMEM((8, rows, inner), BF16),
             pltpu.VMEM((8, rows, inner), BF16),
             pltpu.VMEM((7, rows, inner), BF16),
@@ -537,16 +573,26 @@
             pltpu.VMEM((tokens, width), F32),
             pltpu.VMEM((tokens, width), F32),
             dma, dma, dma, dma((4,)), dma((8,)), dma((8,)), dma((8,)), dma((8,)), dma((8,)), dma((8,)),
-            dma((16, CHUNKS)), dma((8,)), dma((2, 7, SUBS)), dma((8,)), dma((8,)), dma,
+            dma((16, CHUNKS)), dma((8,)), dma((2, 7, SUBS)), dma((8,)), dma((8,)), dma, dma((5,)),
         ],
         compiler_params=pltpu.CompilerParams(
             collective_id=0, has_side_effects=True, vmem_limit_bytes=60 * 1024 * 1024
         ),
     )(
-        query, enc_key, enc_value, ein, looked, dec_gain.astype(F32)[None], cross_query_weight, wo, gain,
+        enc_query, enc_key, enc_value, enc_input, looked, dec_gain[None], cross_query_weight, attn_out_weight,
+        enc_gain.reshape(8, width),
         cross_key_weight, cross_value_weight, cross_out_weight, valid_enc, valid_dec,
     )
-    return keys[None], values[None], decoded.reshape(dec_ids.shape[0], 2, width)
+    return pl.pallas_call(
+        hand_kernel,
+        out_shape=(
+            jax.ShapeDtypeStruct((1, rows, inner), BF16),
+            jax.ShapeDtypeStruct((1, rows, inner), BF16),
+            jax.ShapeDtypeStruct((tokens // 2, 2, width), BF16),
+        ),
+        in_specs=[whole] * 3,
+        out_specs=(whole, whole, whole),
+    )(keys, values, decoded)
 
 
 def chosen(*arrays):

time: 111 us -> 101 us (0.910)
  local copies, waits for them, and re-layouts: 7.77 us -> 3.94 us
  other arithmetic: 3.79 us -> 0 us
  matrix products: 2.34 us -> 0 us
    unnamed x7 -> x1, local copies, waits for them, and re-layouts: 3.9 us -> 0.75 us
    broadcast_in_dim x2 -> x0, other arithmetic: 2.6 us -> none  [the longest x1 1.33 us: local_fused(): lax.dynamic_slice_in_dim(enc_gain, c * width, width, 0).astype(F32)[None]]
    dot_general x2 -> x0, matrix products: 2.34 us -> none  [the longest x1 1.45 us: local_fused(): ein = jnp.dot(turn, enc_input, preferred_element_type=F32).astype(BF16)]
    dynamic_slice x1 -> x0, local copies, waits for them, and re-layouts: 1.87 us -> none  [local_fused(): wo = lax.dynamic_slice_in_dim(attn_out_weight, c * width, width, 1)]
    pallas_call x1, Pallas kernels: 91.4 us -> 89.5 us  [local_fused(): pl.pallas_call(fused_kernel, out_shape=(jax.ShapeDtypeStruct((rows, inner...]
    pallas_call x1 -> x2, Pallas kernels: 3.11 us -> 4.65 us  [the longest x1 2.97 us: local_fused(): pl.pallas_call(pick_kernel, out_shape=(jax.ShapeDtypeStruct((tokens, widt...]
    broadcast_in_dim x0 -> x1, local copies, waits for them, and re-layouts: none -> 1.24 us  [local_fused(): dec_gain[None]]
    convert_element_type x2 -> x0, other arithmetic: 1.18 us -> none  [the longest x1 0.6 us: local_fused(): (jnp.arange(8 * rows, dtype=jnp.int32) < limit).astype(F32)[None]]
where the time goes in v2:
time: 101 us; the launch traced here: 99.4 us
  Pallas kernels  94.2 us (93%)
  local copies, waits for them, and re-layouts  3.94 us (4%)
  between operations  1.29 us (1%)
    pallas_call x1, Pallas kernels, local_fused(): pl.pallas_call(fused_kernel, out_shape=(jax.ShapeDtypeStruct((rows, inner...  89.5 us
    pallas_call x1, Pallas kernels, local_fused(): pl.pallas_call(pick_kernel, out_shape=(jax.ShapeDtypeStruct((tokens, widt...  2.97 us

profile of v2, /device:TPU:0, one launch (start us, length us, event | category | flops | bytes accessed | tf_op | source)
XLA Modules:
  0.0 99.4 jit_solution(13473319302442875019)
XLA Ops:
  1.3 1.2 %broadcast_in_dim.3.dec_gain = bf16[1,512]{1,0:T(2,128)(2,1)} reshape(bf16[512]{0:T(512)(128)(2,1)} %param.25) | data formatting | bytes 2048 | tf_op jit(solution)/shard_map/broadcast_in_dim | solution.py:582
  2.5 1.3 %reshape.13.enc_gain = bf16[8,512]{1,0:T(8,128)(2,1)} reshape(bf16[4096]{0:T(1024)(128)(2,1)} %param.20) | data formatting | bytes 16384 | tf_op jit(solution)/shard_map/reshape | solution.py:583
  3.8 0.8 copy.18
  4.6 0.6 reshape.12.ids_ref
  5.2 3.0 %shard_map.157 = (bf16[32,512]{1,0:T(8,128)(2,1)}, f32[1,1024]{1,0:T(1,128)}, f32[1,128]{1,0:T(1,128)}) custom-call(s32[32]{0:T(128)} %reshape.12.ids_ref, s32[1]{0:T(128)S(6)} %copy.19.length_ref, bf16[16064,512]{1,0:T(8,128)(2,1)} %table_ref.1), custom_call_target="tpu_custom_call" | custom-call | tf_op jit(solution)/shard_map/pallas_call | solution.py:516
  8.2 89.5 %shard_map.158 = (bf16[128,512]{1,0:T(8,128)(2,1)}, bf16[128,512]{1,0:T(8,128)(2,1)}, f32[32,512]{1,0:T(8,128)}) custom-call(bf16[128,512]{1,0:T(8,128)(2,1)} %q.1, bf16[128,512]{1,0:T(8,128)(2,1)} %k.1, bf16[128,512]{1,0:T(8,128)(2,1)} %v.1, bf16[128,4096]{1,0:T(8,128)(2,1)} %ein.1, bf16[32,512]{1,0:T(8,128)(2,1)} %get-tuple-element.9.looked, ...), custom_call_target="tpu_custom_call" | custom-call | tf_op jit(solution)/shard_map/pallas_call | solution.py:533
  97.7 1.7 %shard_map.159 = (bf16[1,128,512]{2,1,0:T(8,128)(2,1)}, bf16[1,128,512]{2,1,0:T(8,128)(2,1)}, bf16[16,2,512]{2,1,0:T(2,128)(2,1)}) custom-call(bf16[128,512]{1,0:T(8,128)(2,1)} %get-tuple-element.12.keys_ref, bf16[128,512]{1,0:T(8,128)(2,1)} %get-tuple-element.13.values_ref, f32[32,512]{1,0:T(8,128)} %get-tuple-element.14.decoded_ref), custom_call_target="tpu_custom_call" | custom-call | tf_op jit(solution)/shard_map/pallas_call | solution.py:586
